TPU v7x, 32 devices: a whole 2x2x4 slice. The times are simulated.
32 devices in a mesh: dp: 8 (over z, core), chan: 4 (over y, x).
Axes of the slice: x: 2, y: 2, z: 4, core: 2. Of those that a mesh axis runs over, the one named last changes fastest.
Arguments:
- images: bfloat16 [16, 16, 16, 2816], P('dp', None, None, 'chan'), may hold values from -6 to 6
- kernel: float32 [7, 7, 2816], P(None, None, 'chan'), may hold values from -0.875 to 0.875
- layernorm_gain: float32 [2816], P('chan'), may hold values from 0.25 to 1.75
- layernorm_bias: float32 [2816], P('chan'), may hold values from -3 to 3
- w_expand: bfloat16 [2816, 11264], P('dp', 'chan'), may hold values from -0.109375 to 0.109375
- w_reduce: bfloat16 [11264, 2816], P('chan', 'dp'), may hold values from -0.0546875 to 0.0546875
- layer_scale: float32 [2816], P('chan'), may hold values from 0.25 to 1
- cotangent: bfloat16 [16, 16, 16, 2816], P('dp', None, None, 'chan'), may hold values from -6 to 6
Outputs:
- output: bfloat16 [16, 16, 16, 2816], P('dp', None, None, 'chan')
- grad_images: bfloat16 [16, 16, 16, 2816], P('dp', None, None, 'chan')
- grad_kernel: float32 [7, 7, 2816], P(None, None, 'chan')
- gain_gradient: float32 [2816], P('chan')
- grad_bias: float32 [2816], P('chan')
- grad_expand: float32 [2816, 11264], P('dp', 'chan')
- grad_reduce: float32 [11264, 2816], P('chan', 'dp')
- grad_scale: float32 [2816], P('chan')
All inputs are finite; a program needn't handle non-finite values.
Results may differ from a plain program's by a relative error of at most 0.025.
Values may be sent and summed in bfloat16 or wider, within the bound.
A program may use at most 128 MiB of HBM per device.

v0:
```python
import math
import jax
import jax.numpy as jnp
from jax import lax
from jax.sharding import PartitionSpec as P

eps = 1e-06


def depthwise(field, kern):
    height = field.shape[1]
    breadth = field.shape[2]
    padded = jnp.pad(field, ((0, 0), (3, 3), (3, 3), (0, 0)))
    total = jnp.zeros(field.shape, jnp.float32)
    for i in range(7):
        for j in range(7):
            total = total + padded[:, i : i + height, j : j + breadth, :] * kern[i, j]
    return total


def normal_cdf(value):
    return 0.5 * (1.0 + jax.scipy.special.erf(value / math.sqrt(2.0)))


def swap_pairs(shift, n):
    return [(i, i ^ shift) for i in range(n)]


def chan_gather(block):
    n = lax.axis_size("chan")
    me = lax.axis_index("chan")
    width = block.shape[1]
    whole = jnp.zeros((block.shape[0], n * width), block.dtype)
    parts = [block] + [lax.ppermute(block, "chan", swap_pairs(k, n)) for k in range(1, n)]
    for k in range(n):
        whole = lax.dynamic_update_slice(whole, parts[k], (0, (me ^ k) * width))
    return whole


def chan_scatter(partial):
    n = lax.axis_size("chan")
    me = lax.axis_index("chan")
    width = partial.shape[1] // n
    total = lax.dynamic_slice_in_dim(partial, me * width, width, 1).astype(jnp.float32)
    for k in range(1, n):
        mine = lax.dynamic_slice_in_dim(partial, (me ^ k) * width, width, 1)
        total = total + lax.ppermute(mine, "chan", swap_pairs(k, n)).astype(jnp.float32)
    return total


def dp_scatter(partial):
    return lax.psum_scatter(partial, "dp", scatter_dimension=0, tiled=True)


def dp_total(value):
    n = lax.axis_size("dp")
    shift = 1
    while shift < n:
        value = value + lax.ppermute(value, "dp", swap_pairs(shift, n))
        shift *= 2
    return value


def body(
    images, kernel, layernorm_gain, layernorm_bias, w_expand, w_reduce, layer_scale, cotangent
):
    shape_in = images.shape
    height = shape_in[1]
    breadth = shape_in[2]
    positions = shape_in[0] * height * breadth
    local_chan = shape_in[3]
    image_width = local_chan * lax.axis_size("chan")
    xf = images.astype(jnp.float32)
    conv = depthwise(xf, kernel).reshape(positions, local_chan)
    mean_val = lax.psum(jnp.sum(conv, axis=1), "chan")[:, None] / image_width
    centred_rows = conv - mean_val
    var = lax.psum(jnp.sum(centred_rows * centred_rows, axis=1), "chan")[:, None] / image_width
    inverse_deviation = lax.rsqrt(var + eps)
    standardized_input = centred_rows * inverse_deviation
    normed_output = (standardized_input * layernorm_gain + layernorm_bias).astype(jnp.bfloat16)
    normed_all = chan_gather(normed_output)
    expand_all = lax.all_gather(w_expand, "dp", axis=0, tiled=True)
    pre = jnp.dot(normed_all, expand_all, preferred_element_type=jnp.float32)
    hidden = (pre * normal_cdf(pre)).astype(jnp.bfloat16)
    dyf = cotangent.astype(jnp.float32).reshape(positions, local_chan)
    dbranch = (dyf * layer_scale).astype(jnp.bfloat16)
    dbranch_all = chan_gather(dbranch)
    reduce_part = lax.dot_general(
        dbranch_all, hidden, (((0,), (0,)), ((), ())), preferred_element_type=jnp.float32
    ).astype(jnp.bfloat16)
    reduce_all = lax.all_gather(w_reduce, "dp", axis=1, tiled=True)
    reduce_part, reduce_all = lax.optimization_barrier((reduce_part, reduce_all))
    grad_reduce = dp_scatter(reduce_part).astype(jnp.float32).T
    dhidden = lax.dot_general(
        dbranch_all, reduce_all, (((1,), (1,)), ((), ())), preferred_element_type=jnp.float32
    )
    slope = normal_cdf(pre) + pre * jnp.exp(-0.5 * pre * pre) / math.sqrt(2.0 * math.pi)
    dpre = (dhidden * slope).astype(jnp.bfloat16)
    expand_part = lax.dot_general(
        normed_all, dpre, (((0,), (0,)), ((), ())), preferred_element_type=jnp.float32
    ).astype(jnp.bfloat16)
    expand_part, dpre, hidden, reduce_all = lax.optimization_barrier(
        (expand_part, dpre, hidden, reduce_all)
    )
    grad_expand = dp_scatter(expand_part).astype(jnp.float32)
    partial_normed = lax.dot_general(
        dpre, expand_all, (((1,), (1,)), ((), ())), preferred_element_type=jnp.float32
    )
    normed_grad = chan_scatter(partial_normed.astype(jnp.bfloat16))
    partial_branch = jnp.dot(hidden, reduce_all, preferred_element_type=jnp.float32)
    branch = chan_scatter(partial_branch.astype(jnp.bfloat16))
    xr = xf.reshape(positions, local_chan)
    output = (xr + layer_scale * branch).astype(jnp.bfloat16).reshape(shape_in)
    scale_part = jnp.sum(dyf * branch, axis=0)
    gain_partial = jnp.sum(normed_grad * standardized_input, axis=0)
    bias_part = jnp.sum(normed_grad, axis=0)
    standardized_grad = normed_grad * layernorm_gain
    first_half, second_half = lax.psum(
        (
            jnp.sum(standardized_grad, axis=1),
            jnp.sum(standardized_grad * standardized_input, axis=1),
        ),
        "chan",
    )
    conv_output_grad = inverse_deviation * (
        standardized_grad
        - first_half[:, None] / image_width
        - standardized_input * (second_half[:, None] / image_width)
    )
    conv_output_grad = conv_output_grad.reshape(shape_in)
    padded = jnp.pad(xf, ((0, 0), (3, 3), (3, 3), (0, 0)))
    dpad = jnp.pad(conv_output_grad, ((0, 0), (3, 3), (3, 3), (0, 0)))
    back = cotangent.astype(jnp.float32)
    kern_rows = []
    for i in range(7):
        tap_row = []
        for j in range(7):
            tap_row.append(
                jnp.sum(
                    padded[:, i : i + height, j : j + breadth, :] * conv_output_grad, axis=(0, 1, 2)
                )
            )
            back = back + dpad[:, 6 - i : 6 - i + height, 6 - j : 6 - j + breadth, :] * kernel[i, j]
        kern_rows.append(jnp.stack(tap_row))
    kernel_part = jnp.stack(kern_rows)
    grad_images = back.astype(jnp.bfloat16)
    small = dp_total(
        jnp.concatenate(
            [
                kernel_part.reshape(-1, local_chan),
                gain_partial[None],
                bias_part[None],
                scale_part[None],
            ]
        )
    )
    taps = kernel_part.shape[0] * kernel_part.shape[1]
    grad_kernel = small[:taps].reshape(kernel_part.shape)
    gain_gradient, grad_bias, grad_scale = (small[taps], small[taps + 1], small[taps + 2])
    return (
        output,
        grad_images,
        grad_kernel,
        gain_gradient,
        grad_bias,
        grad_expand,
        grad_reduce,
        grad_scale,
    )


def solution(mesh):
    in_specs = (
        P("dp", None, None, "chan"),
        P(None, None, "chan"),
        P("chan"),
        P("chan"),
        P("dp", "chan"),
        P("chan", "dp"),
        P("chan"),
        P("dp", None, None, "chan"),
    )
    out_specs = (
        P("dp", None, None, "chan"),
        P("dp", None, None, "chan"),
        P(None, None, "chan"),
        P("chan"),
        P("chan"),
        P("dp", "chan"),
        P("chan", "dp"),
        P("chan"),
    )
    return jax.shard_map(body, mesh=mesh, in_specs=in_specs, out_specs=out_specs, check_vma=False)
```

profile of v0, /device:TPU:0, one launch (start us, length us, event | category | flops | bytes accessed | tf_op | source)
XLA Modules:
  0.0 632.4 jit_solution(10809469362754886029)
XLA Ops:
  10.0 12.3 %fusion.108 = (f32[2,16,16]{2,1,0:T(8,128)S(1)}, f32[2,16,16,704]{3,2,1,0:T(8,128)S(1)}) fusion(f32[704]{0:T(1024)S(1)} %get-tuple-element.123, f32[704]{0:T(1024)S(1)} %get-tuple-element.124, f32[704]{0:T(1024)S(1)} %get-tuple-element.77, f32[704]{0:T(1024)S(1)} %get-tuple-element.78, f32[704]{0:T(1024)S(1)} %get-tuple-element.79, ...), kind=kLoop, calls=%fused_computation.344 | loop fusion | flops 35323392 | bytes 3023616 | tf_op jit(solution)/shard_map/reduce_sum | solution.py:75
  22.4 11.3 %psum.28 = f32[512]{0:T(512)S(1)} all-reduce(f32[512]{0:T(512)S(1)} %reduce_sum.509), channel_id=1, replica_groups=mesh['dp'=8,'chan'=4] {'chan'}, use_global_device_ids=true, to_apply=%region_1.2 | all-reduce | flops 512 | bytes 4096 | tf_op jit(solution)/shard_map/psum | solution.py:75
  34.2 7.9 %psum.29 = f32[512]{0:T(512)S(1)} all-reduce(f32[512]{0:T(512)S(1)} %reduce_sum.511), channel_id=1, replica_groups=mesh['dp'=8,'chan'=4] {'chan'}, use_global_device_ids=true, to_apply=%region_3.4 | all-reduce | flops 512 | bytes 4096 | tf_op jit(solution)/shard_map/psum | solution.py:77
  55.7 9.3 %collective-permute-done = bf16[512,704]{0,1:T(8,128)(2,1)} collective-permute-done((bf16[512,704]{0,1:T(8,128)(2,1)}, bf16[512,704]{0,1:T(8,128)(2,1)}, u32[]{:S(2)}, u32[]{:S(2)}) %collective-permute-start) | collective-permute-done | bytes 720928 | tf_op jit(solution)/shard_map/ppermute | solution.py:34
  68.3 8.1 %dynamic_update_slice.24 = bf16[512,2816]{1,0:T(8,128)(2,1)} dynamic-update-slice(bf16[512,2816]{1,0:T(8,128)(2,1)} %broadcast.39.clone, bf16[512,704]{1,0:T(8,128)(2,1)} %add_convert_fusion, s32[]{:T(128)} %constant.11.clone.1, s32[]{:T(128)S(6)} %select_n.8) | dynamic-update-slice | bytes 1441796 | tf_op jit(solution)/shard_map/dynamic_update_slice | solution.py:36
  78.2 8.1 %dynamic_update_slice.28 = bf16[512,2816]{1,0:T(8,128)(2,1)} dynamic-update-slice(bf16[512,2816]{1,0:T(8,128)(2,1)} %broadcast.39.clone.1, bf16[512,704]{1,0:T(8,128)(2,1)} %fusion.104, s32[]{:T(128)} %constant.11.clone.1, s32[]{:T(128)S(6)} %select_n.8) | dynamic-update-slice | bytes 1441796 | tf_op jit(solution)/shard_map/dynamic_update_slice | solution.py:36
  88.6 9.0 %dynamic_update_slice.25 = bf16[512,2816]{1,0:T(8,128)(2,1)} dynamic-update-slice(bf16[512,2816]{1,0:T(8,128)(2,1)} %dynamic_update_slice.24, bf16[512,704]{1,0:T(8,128)(2,1)} %copy.17, s32[]{:T(128)} %constant.11.clone.1, s32[]{:T(128)S(6)} %select_n.9) | dynamic-update-slice | bytes 1441796 | tf_op jit(solution)/shard_map/dynamic_update_slice | solution.py:36
  99.8 9.0 %dynamic_update_slice.29 = bf16[512,2816]{1,0:T(8,128)(2,1)} dynamic-update-slice(bf16[512,2816]{1,0:T(8,128)(2,1)} %dynamic_update_slice.28, bf16[512,704]{1,0:T(8,128)(2,1)} %copy.23, s32[]{:T(128)} %constant.11.clone.1, s32[]{:T(128)S(6)} %select_n.9) | dynamic-update-slice | bytes 1441796 | tf_op jit(solution)/shard_map/dynamic_update_slice | solution.py:36
  111.1 8.1 %dynamic_update_slice.26 = bf16[512,2816]{1,0:T(8,128)(2,1)} dynamic-update-slice(bf16[512,2816]{1,0:T(8,128)(2,1)} %dynamic_update_slice.25, bf16[512,704]{1,0:T(8,128)(2,1)} %copy.19, s32[]{:T(128)} %constant.11.clone.1, s32[]{:T(128)S(6)} %select_n.10) | dynamic-update-slice | bytes 1441796 | tf_op jit(solution)/shard_map/dynamic_update_slice | solution.py:36
  121.4 8.1 %dynamic_update_slice.30 = bf16[512,2816]{1,0:T(8,128)(2,1)} dynamic-update-slice(bf16[512,2816]{1,0:T(8,128)(2,1)} %dynamic_update_slice.29, bf16[512,704]{1,0:T(8,128)(2,1)} %copy.25, s32[]{:T(128)} %constant.11.clone.1, s32[]{:T(128)S(6)} %select_n.10) | dynamic-update-slice | bytes 1441796 | tf_op jit(solution)/shard_map/dynamic_update_slice | solution.py:36
  131.8 8.3 %dynamic_update_slice.27 = bf16[512,2816]{1,0:T(8,128)(2,1)} dynamic-update-slice(bf16[512,2816]{1,0:T(8,128)(2,1)} %dynamic_update_slice.26, bf16[512,704]{1,0:T(8,128)(2,1)} %copy.21, s32[]{:T(128)} %constant.11.clone.1, s32[]{:T(128)S(6)} %select_n.11) | dynamic-update-slice | bytes 1441796 | tf_op jit(solution)/shard_map/dynamic_update_slice | solution.py:36
  142.4 8.3 %dynamic_update_slice.31 = bf16[512,2816]{1,0:T(8,128)(2,1)} dynamic-update-slice(bf16[512,2816]{1,0:T(8,128)(2,1)} %dynamic_update_slice.30, bf16[512,704]{1,0:T(8,128)(2,1)} %copy.27, s32[]{:T(128)} %constant.11.clone.1, s32[]{:T(128)S(6)} %select_n.11) | dynamic-update-slice | bytes 1441796 | tf_op jit(solution)/shard_map/dynamic_update_slice | solution.py:36
  156.0 15.2 %multiply_convert_fusion = (bf16[512,2816]{1,0:T(8,128)(2,1)S(1)}, f32[512,2816]{1,0:T(8,128)}) fusion(bf16[512,2816]{1,0:T(8,128)(2,1)} %dynamic_update_slice.27, bf16[2816,2816]{1,0:T(8,128)(2,1)} %all-gather.3.cloned.1.call-done), kind=kOutput, calls=%fused_computation.105 | convolution fusion | flops 8127381504 | bytes 27394048 | tf_op jit(solution)/shard_map/dot_general | solution.py:83
  172.8 12.4 %convolution_convert_fusion.1 = bf16[2816,2816]{1,0:T(8,128)(2,1)} fusion(bf16[512,2816]{1,0:T(8,128)(2,1)S(1)} %copy-done.7, bf16[512,2816]{1,0:T(8,128)(2,1)S(1)} %get-tuple-element.15), kind=kOutput, calls=%fused_computation.97 | convolution fusion | flops 8128102400 | bytes 21626880 | tf_op jit(solution)/shard_map/dot_general | solution.py:88
  185.1 114.3 %all-gather.5.cloned.1.call-done = bf16[2816,2816]{0,1:T(8,128)(2,1)} async-done(((bf16[2816,352]{0,1:T(8,128)(2,1)}), bf16[2816,2816]{0,1:T(8,128)(2,1)}) %all-gather.5.cloned.1.call-update) | async-done | bytes 15859728 | tf_op jit(solution)/shard_map/all_gather | solution.py:91
  299.6 15.3 %fusion.5 = bf16[512,2816]{1,0:T(8,128)(2,1)S(1)} fusion(f32[512,2816]{1,0:T(8,128)} %get-tuple-element.140, bf16[512,2816]{1,0:T(8,128)(2,1)} %dynamic_update_slice.31, bf16[2816,2816]{0,1:T(8,128)(2,1)} %all-gather.5.cloned.1.call-done), kind=kOutput, calls=%fused_computation.104 | convolution fusion | flops 8134590464 | bytes 27394048 | tf_op jit(solution)/shard_map/dot_general | solution.py:94
  316.4 11.9 %convolution_convert_fusion = bf16[2816,2816]{1,0:T(8,128)(2,1)} fusion(bf16[512,2816]{1,0:T(8,128)(2,1)S(1)} %copy-done.8, bf16[512,2816]{1,0:T(8,128)(2,1)S(1)} %fusion.5), kind=kOutput, calls=%fused_computation.96 | convolution fusion | flops 8128102400 | bytes 21626880 | tf_op jit(solution)/shard_map/dot_general | solution.py:99
  328.3 13.7 %convolution_convert_fusion.3 = bf16[512,2816]{1,0:T(8,128)(2,1)S(1)} fusion(bf16[512,2816]{1,0:T(8,128)(2,1)} %copy-done.13, bf16[2816,2816]{0,1:T(8,128)(2,1)} %all-gather.5.cloned.1.call-done), kind=kOutput, calls=%fused_computation.108 | convolution fusion | flops 8121614336 | bytes 21626880 | tf_op jit(solution)/shard_map/dot_general | solution.py:110
  355.1 13.5 %convolution_convert_fusion.2 = bf16[512,2816]{1,0:T(8,128)(2,1)S(1)} fusion(bf16[512,2816]{1,0:T(8,128)(2,1)} %copy-done.14, bf16[2816,2816]{1,0:T(8,128)(2,1)} %all-gather.3.cloned.1.call-done), kind=kOutput, calls=%fused_computation.107 | convolution fusion | flops 8121614336 | bytes 21626880 | tf_op jit(solution)/shard_map/dot_general | solution.py:106
  394.7 21.8 %collective-permute-done.10 = bf16[512,704]{0,1:T(8,128)(2,1)} collective-permute-done((bf16[512,704]{0,1:T(8,128)(2,1)}, bf16[512,704]{0,1:T(8,128)(2,1)}, u32[]{:S(2)}, u32[]{:S(2)}) %collective-permute-start.10) | collective-permute-done | bytes 720928 | tf_op jit(solution)/shard_map/ppermute | solution.py:47
  429.0 10.0 %all-reduce.2 = (f32[512]{0:T(512)S(1)}, f32[512]{0:T(512)S(1)}) all-reduce(f32[512]{0:T(512)S(1)} %get-tuple-element.143, f32[512]{0:T(512)S(1)} %get-tuple-element.142), channel_id=1, replica_groups=mesh['dp'=8,'chan'=4] {'chan'}, use_global_device_ids=true, to_apply=%region_7.8 | all-reduce | flops 1024 | bytes 8192 | tf_op jit(solution)/shard_map/psum | solution.py:118
  455.2 6.7 %collective-permute-done.13 = f32[52,704]{1,0:T(8,128)S(1)} collective-permute-done((f32[52,704]{1,0:T(8,128)S(1)}, f32[52,704]{1,0:T(8,128)S(1)}, u32[]{:S(2)}, u32[]{:S(2)}) %collective-permute-start.13) | collective-permute-done | bytes 146464 | tf_op jit(solution)/shard_map/ppermute | solution.py:59
  462.9 12.3 %fusion.99 = bf16[2,16,16,704]{3,2,1,0:T(8,128)(2,1)} fusion(f32[2,16,16,704]{3,2,1,0:T(8,128)S(1)} %bitcast.104, bf16[2,16,16,704]{3,2,1,0:T(8,128)(2,1)S(1)} %copy-done.2, f32[704]{0:T(1024)S(1)} %get-tuple-element.123, f32[704]{0:T(1024)S(1)} %get-tuple-element.124, f32[704]{0:T(1024)S(1)} %get-tuple-element.77, f32[704]{0:T(1024)S(1)} %get-tuple-element.78, ...), kind=kLoop, calls=%fused_computation.203 | loop fusion | flops 36044800 | bytes 3021568 | tf_op jit(solution)/shard_map/convert_element_type | solution.py:146
  480.3 141.6 %reduce-scatter.3.cloned.1.call-done = bf16[352,2816]{1,0:T(8,128)(2,1)} async-done(((bf16[2816,2816]{1,0:T(8,128)(2,1)}), bf16[352,2816]{1,0:T(8,128)(2,1)}) %reduce-scatter.3.cloned.1.call-update) | async-done | bytes 1982480 | tf_op jit(solution)/shard_map/reduce_scatter | solution.py:52
  (184 shorter events, 121.1 us)
Async XLA Ops:
  7.2 148.8 %all-gather.3.cloned.1.call-start = ((), (), s32[]{:S(2)}) async-start(), calls=%async_computation.2 | async-start | bytes 17842176 | tf_op jit(solution)/shard_map/all_gather | solution.py:82
  7.9 291.6 %all-gather.5.cloned.1.call-start = ((), (), s32[]{:S(2)}) async-start(), calls=%async_computation.3 | async-start | bytes 17842176 | tf_op jit(solution)/shard_map/all_gather | solution.py:91
  8.7 467.9 %reduce-scatter.5.cloned.1.call-start = ((), (), s32[]{:S(2)}) async-start(), calls=%async_computation.5 | async-start | bytes 17842176 | tf_op jit(solution)/shard_map/reduce_scatter | solution.py:52
  22.3 19.9 %copy-start.10 = (f32[704]{0:T(1024)S(1)}, f32[704]{0:T(1024)}, u32[]{:S(2)}) copy-start(f32[704]{0:T(1024)} %param.10) | copy-start | bytes 8452
  22.3 19.9 %copy-start.12 = (f32[704]{0:T(1024)S(1)}, f32[704]{0:T(1024)}, u32[]{:S(2)}) copy-start(f32[704]{0:T(1024)} %param.11) | copy-start | bytes 8452
  45.6 19.4 %collective-permute-start = (bf16[512,704]{0,1:T(8,128)(2,1)}, bf16[512,704]{0,1:T(8,128)(2,1)}, u32[]{:S(2)}, u32[]{:S(2)}) collective-permute-start(bf16[512,704]{0,1:T(8,128)(2,1)} %copy.16), channel_id=1, source_target_pairs={{0,1},{1,0},{2,3},{3,2},{4,5},{5,4},{6,7},{7,6},{8,9},{9,8},{10,11... | collective-permute-start | bytes 2162696 | tf_op jit(solution)/shard_map/ppermute | solution.py:34
  51.5 46.0 %collective-permute-start.3 = (bf16[512,704]{0,1:T(8,128)(2,1)}, bf16[512,704]{0,1:T(8,128)(2,1)}, u32[]{:S(2)}, u32[]{:S(2)}) collective-permute-start(bf16[512,704]{0,1:T(8,128)(2,1)} %copy.22), channel_id=1, source_target_pairs={{0,1},{1,0},{2,3},{3,2},{4,5},{5,4},{6,7},{7,6},{8,9},{9,8},{10,11... | collective-permute-start | bytes 2162696 | tf_op jit(solution)/shard_map/ppermute | solution.py:34
  52.2 56.7 %collective-permute-start.1 = (bf16[512,704]{0,1:T(8,128)(2,1)}, bf16[512,704]{0,1:T(8,128)(2,1)}, u32[]{:S(2)}, u32[]{:S(2)}) collective-permute-start(bf16[512,704]{0,1:T(8,128)(2,1)} %copy.16), channel_id=1, source_target_pairs={{0,2},{1,3},{2,0},{3,1},{4,6},{5,7},{6,4},{7,5},{8,10},{9,11},{10,... | collective-permute-start | bytes 2162696 | tf_op jit(solution)/shard_map/ppermute | solution.py:34
  52.7 66.5 %collective-permute-start.4 = (bf16[512,704]{0,1:T(8,128)(2,1)}, bf16[512,704]{0,1:T(8,128)(2,1)}, u32[]{:S(2)}, u32[]{:S(2)}) collective-permute-start(bf16[512,704]{0,1:T(8,128)(2,1)} %copy.22), channel_id=1, source_target_pairs={{0,2},{1,3},{2,0},{3,1},{4,6},{5,7},{6,4},{7,5},{8,10},{9,11},{10,... | collective-permute-start | bytes 2162696 | tf_op jit(solution)/shard_map/ppermute | solution.py:34
  54.2 75.3 %collective-permute-start.2 = (bf16[512,704]{0,1:T(8,128)(2,1)}, bf16[512,704]{0,1:T(8,128)(2,1)}, u32[]{:S(2)}, u32[]{:S(2)}) collective-permute-start(bf16[512,704]{0,1:T(8,128)(2,1)} %copy.16), channel_id=1, source_target_pairs={{0,3},{1,2},{2,1},{3,0},{4,7},{5,6},{6,5},{7,4},{8,11},{9,10},{10,... | collective-permute-start | bytes 2162696 | tf_op jit(solution)/shard_map/ppermute | solution.py:34
  65.0 75.1 %collective-permute-start.5 = (bf16[512,704]{0,1:T(8,128)(2,1)}, bf16[512,704]{0,1:T(8,128)(2,1)}, u32[]{:S(2)}, u32[]{:S(2)}) collective-permute-start(bf16[512,704]{0,1:T(8,128)(2,1)} %copy.22), channel_id=1, source_target_pairs={{0,3},{1,2},{2,1},{3,0},{4,7},{5,6},{6,5},{7,4},{8,11},{9,10},{10,... | collective-permute-start | bytes 2162696 | tf_op jit(solution)/shard_map/ppermute | solution.py:34
  156.0 16.8 %copy-start.7 = (bf16[512,2816]{1,0:T(8,128)(2,1)S(1)}, bf16[512,2816]{1,0:T(8,128)(2,1)}, u32[]{:S(2)}) copy-start(bf16[512,2816]{1,0:T(8,128)(2,1)} %dynamic_update_slice.31) | copy-start | bytes 8650756
  299.5 322.4 %reduce-scatter.3.cloned.1.call-start = ((), (), s32[]{:S(2)}) async-start(), calls=%async_computation.4 | async-start | bytes 17842176 | tf_op jit(solution)/shard_map/reduce_scatter | solution.py:52
  299.5 16.8 %copy-start.8 = (bf16[512,2816]{1,0:T(8,128)(2,1)S(1)}, bf16[512,2816]{1,0:T(8,128)(2,1)}, u32[]{:S(2)}) copy-start(bf16[512,2816]{1,0:T(8,128)(2,1)} %dynamic_update_slice.27) | copy-start | bytes 8650756
  351.7 34.7 %collective-permute-start.7 = (bf16[512,704]{0,1:T(8,128)(2,1)}, bf16[512,704]{0,1:T(8,128)(2,1)}, u32[]{:S(2)}, u32[]{:S(2)}) collective-permute-start(bf16[512,704]{0,1:T(8,128)(2,1)} %copy.30), channel_id=1, source_target_pairs={{0,2},{1,3},{2,0},{3,1},{4,6},{5,7},{6,4},{7,5},{8,10},{9,11},{10,... | collective-permute-start | bytes 2162696 | tf_op jit(solution)/shard_map/ppermute | solution.py:47
  353.1 37.0 %collective-permute-start.8 = (bf16[512,704]{0,1:T(8,128)(2,1)}, bf16[512,704]{0,1:T(8,128)(2,1)}, u32[]{:S(2)}, u32[]{:S(2)}) collective-permute-start(bf16[512,704]{0,1:T(8,128)(2,1)} %copy.32), channel_id=1, source_target_pairs={{0,3},{1,2},{2,1},{3,0},{4,7},{5,6},{6,5},{7,4},{8,11},{9,10},{10,... | collective-permute-start | bytes 2162696 | tf_op jit(solution)/shard_map/ppermute | solution.py:47
  354.6 37.8 %collective-permute-start.6 = (bf16[512,704]{0,1:T(8,128)(2,1)}, bf16[512,704]{0,1:T(8,128)(2,1)}, u32[]{:S(2)}, u32[]{:S(2)}) collective-permute-start(bf16[512,704]{0,1:T(8,128)(2,1)} %copy.28), channel_id=1, source_target_pairs={{0,1},{1,0},{2,3},{3,2},{4,5},{5,4},{6,7},{7,6},{8,9},{9,8},{10,11... | collective-permute-start | bytes 2162696 | tf_op jit(solution)/shard_map/ppermute | solution.py:47
  376.1 40.5 %collective-permute-start.10 = (bf16[512,704]{0,1:T(8,128)(2,1)}, bf16[512,704]{0,1:T(8,128)(2,1)}, u32[]{:S(2)}, u32[]{:S(2)}) collective-permute-start(bf16[512,704]{0,1:T(8,128)(2,1)} %copy.36), channel_id=1, source_target_pairs={{0,2},{1,3},{2,0},{3,1},{4,6},{5,7},{6,4},{7,5},{8,10},{9,11},{10,... | collective-permute-start | bytes 2162696 | tf_op jit(solution)/shard_map/ppermute | solution.py:47
  379.8 39.1 %collective-permute-start.11 = (bf16[512,704]{0,1:T(8,128)(2,1)}, bf16[512,704]{0,1:T(8,128)(2,1)}, u32[]{:S(2)}, u32[]{:S(2)}) collective-permute-start(bf16[512,704]{0,1:T(8,128)(2,1)} %copy.38), channel_id=1, source_target_pairs={{0,3},{1,2},{2,1},{3,0},{4,7},{5,6},{6,5},{7,4},{8,11},{9,10},{10,... | collective-permute-start | bytes 2162696 | tf_op jit(solution)/shard_map/ppermute | solution.py:47
  386.4 34.8 %collective-permute-start.9 = (bf16[512,704]{0,1:T(8,128)(2,1)}, bf16[512,704]{0,1:T(8,128)(2,1)}, u32[]{:S(2)}, u32[]{:S(2)}) collective-permute-start(bf16[512,704]{0,1:T(8,128)(2,1)} %copy.34), channel_id=1, source_target_pairs={{0,1},{1,0},{2,3},{3,2},{4,5},{5,4},{6,7},{7,6},{8,9},{9,8},{10,11... | collective-permute-start | bytes 2162696 | tf_op jit(solution)/shard_map/ppermute | solution.py:47
  452.7 10.3 %copy-start.1 = (f32[512,704]{1,0:T(8,128)S(1)}, f32[512,704]{1,0:T(8,128)}, u32[]{:S(2)}) copy-start(f32[512,704]{1,0:T(8,128)} %copy-done) | copy-start | bytes 4325380
  453.6 1.5 collective-permute-start.12
  455.1 6.7 %collective-permute-start.13 = (f32[52,704]{1,0:T(8,128)S(1)}, f32[52,704]{1,0:T(8,128)S(1)}, u32[]{:S(2)}, u32[]{:S(2)}) collective-permute-start(f32[52,704]{1,0:T(8,128)S(1)} %fusion.121), channel_id=1, source_target_pairs={{0,8},{4,12},{8,0},{12,4},{16,24},{20,28},{24,16},{28,20},{1,9},{5... | collective-permute-start | bytes 439304 | tf_op jit(solution)/shard_map/ppermute | solution.py:59
  461.8 13.4 %collective-permute-start.14 = (f32[52,704]{1,0:T(8,128)S(1)}, f32[52,704]{1,0:T(8,128)S(1)}, u32[]{:S(2)}, u32[]{:S(2)}) collective-permute-start(f32[52,704]{1,0:T(8,128)S(1)} %add.498), channel_id=1, source_target_pairs={{0,16},{4,20},{8,24},{12,28},{16,0},{20,4},{24,8},{28,12},{1,17},{... | collective-permute-start | bytes 439304 | tf_op jit(solution)/shard_map/ppermute | solution.py:59
  (10 other events, 34.9 us)
Sparse Core Ops, SparseCore 0:
  9.7 146.2 all-gather.2
  157.6 141.8 all-gather.4
  301.8 157.9 reduce-scatter.4
  462.0 159.8 reduce-scatter.2
where the time goes:
time: 644 us; the launch traced here: 632 us
  waiting for transfers between devices  307 us (48%)
  local copies, waits for them, and re-layouts  128 us (20%)
  matrix products  82 us (13%)
  other arithmetic  54.9 us (9%)
  blocking collectives  29.2 us (5%)
  starting transfers between devices  16.5 us (3%)
  between operations  14.7 us (2%)
    reduce_scatter x2, waiting for transfers between devices, dp_scatter(): return lax.psum_scatter(partial, 'dp', scatter_dimension=0, tiled=True)  142 us
    all_gather x1, waiting for transfers between devices, body(): reduce_all = lax.all_gather(w_reduce, 'dp', axis=1, tiled=True)  114 us
    dynamic_update_slice x8, local copies, waits for them, and re-layouts, chan_gather(): whole = lax.dynamic_update_slice(whole, parts[k], (0, (me ^ k) * width))  67.1 us
    ppermute x6, waiting for transfers between devices, chan_scatter(): lax.ppermute(mine, 'chan', swap_pairs(k, n)).astype(jnp.float32)  26.9 us
    dynamic_slice x8, local copies, waits for them, and re-layouts, chan_scatter(): mine = lax.dynamic_slice_in_dim(partial, (me ^ k) * width, width, 1)  19.2 us
    dot_general x1, matrix products, body(): lax.dot_general(dbranch_all, reduce_all, (((1,), (1,)), ((), ())), prefer...  15.3 us
    dot_general x1, matrix products, body(): pre = jnp.dot(normed_all, expand_all, preferred_element_type=jnp.float32)  15.2 us
    ppermute x6, local copies, waits for them, and re-layouts, chan_scatter(): lax.ppermute(mine, 'chan', swap_pairs(k, n)).astype(jnp.float32)  13.8 us
  transfers between devices with their start and end apart: 19, of which 8 were waited for; matrix products, arithmetic and copies ran while one was open for 41% of the time, Pallas kernels for 0%

commit v1 on v0

--- a/solution.py
+++ b/solution.py
@@ -5,6 +5,19 @@
 from jax.sharding import PartitionSpec as P
 
 eps = 1e-06
+
+
+def collect(value, axis, dim):
+    ways = lax.axis_size(axis)
+    up = [(d, (d + 1) % ways) for d in range(ways)]
+    down = [(d, (d - 1) % ways) for d in range(ways)]
+    earlier, later = ([value], [value])
+    for _ in range(ways // 2):
+        earlier.append(lax.ppermute(earlier[-1], axis, up))
+    for _ in range((ways - 1) // 2):
+        later.append(lax.ppermute(later[-1], axis, down))
+    line = jnp.concatenate([*earlier[::-1], *later[1:]], axis=dim)
+    return jnp.roll(line, (lax.axis_index(axis) - ways // 2) * value.shape[dim], axis=dim)
 
 
 def depthwise(field, kern):
@@ -88,7 +101,7 @@
     reduce_part = lax.dot_general(
         dbranch_all, hidden, (((0,), (0,)), ((), ())), preferred_element_type=jnp.float32
     ).astype(jnp.bfloat16)
-    reduce_all = lax.all_gather(w_reduce, "dp", axis=1, tiled=True)
+    reduce_all = collect(w_reduce, "dp", 1)
     reduce_part, reduce_all = lax.optimization_barrier((reduce_part, reduce_all))
     grad_reduce = dp_scatter(reduce_part).astype(jnp.float32).T
     dhidden = lax.dot_general(

time: 644 us -> 787 us (1.22)
  waiting for transfers between devices: 307 us -> 386 us
  starting transfers between devices: 16.5 us -> 77.7 us
    ppermute x0 -> x7, waiting for transfers between devices: none -> 169 us  [the longest x4 158 us: collect(): earlier.append(lax.ppermute(earlier[-1], axis, up))]
    all_gather x1 -> x0, waiting for transfers between devices: 114 us -> none  [body(): reduce_all = lax.all_gather(w_reduce, 'dp', axis=1, tiled=True)]
    ppermute x0 -> x7, starting transfers between devices: none -> 37.2 us  [the longest x4 25.6 us: collect(): earlier.append(lax.ppermute(earlier[-1], axis, up))]
    ppermute x3, starting transfers between devices: 1.25 us -> 24.8 us  [dp_total(): value = value + lax.ppermute(value, 'dp', swap_pairs(shift, n))]
    unnamed x36 -> x215, local copies, waits for them, and re-layouts: 3.88 us -> 27.3 us
    reduce_scatter x2, waiting for transfers between devices: 142 us -> 157 us  [dp_scatter(): return lax.psum_scatter(partial, 'dp', scatter_dimension=0, tiled=True)]
    dynamic_slice x8, local copies, waits for them, and re-layouts: 19.2 us -> 7.31 us  [chan_scatter(): mine = lax.dynamic_slice_in_dim(partial, (me ^ k) * width, width, 1)]
    dynamic_slice x0 -> x1, local copies, waits for them, and re-layouts: none -> 7.91 us  [collect(): jnp.roll(line, (lax.axis_index(axis) - ways // 2) * value.shape[dim], axi...]
  transfers between devices with their start and end apart: 19 -> 25, of which waited for: 8 -> 11; matrix products, arithmetic and copies ran while one was open for 41% -> 30% of each run, Pallas kernels for 0% -> 0%
where the time goes in v1:
time: 787 us; the launch traced here: 776 us
  waiting for transfers between devices  386 us (49%)
  local copies, waits for them, and re-layouts  133 us (17%)
  matrix products  80.1 us (10%)
  starting transfers between devices  77.7 us (10%)
  other arithmetic  55.9 us (7%)
  blocking collectives  27.4 us (3%)
  between operations  16 us (2%)
    ppermute x4, waiting for transfers between devices, collect(): earlier.append(lax.ppermute(earlier[-1], axis, up))  158 us
    reduce_scatter x2, waiting for transfers between devices, dp_scatter(): return lax.psum_scatter(partial, 'dp', scatter_dimension=0, tiled=True)  157 us
    dynamic_update_slice x8, local copies, waits for them, and re-layouts, chan_gather(): whole = lax.dynamic_update_slice(whole, parts[k], (0, (me ^ k) * width))  64.4 us
    ppermute x6, waiting for transfers between devices, chan_scatter(): lax.ppermute(mine, 'chan', swap_pairs(k, n)).astype(jnp.float32)  28.4 us
    unnamed x215, local copies, waits for them, and re-layouts  27.3 us
    ppermute x4, starting transfers between devices, collect(): earlier.append(lax.ppermute(earlier[-1], axis, up))  25.6 us
    ppermute x3, starting transfers between devices, dp_total(): value = value + lax.ppermute(value, 'dp', swap_pairs(shift, n))  24.8 us
    ppermute x6, waiting for transfers between devices, chan_gather(): lax.ppermute(block, 'chan', swap_pairs(k, n))  16.7 us
  transfers between devices with their start and end apart: 25, of which 11 were waited for; matrix products, arithmetic and copies ran while one was open for 30% of the time, Pallas kernels for 0%

profile of v1, /device:TPU:0, one launch (start us, length us, event | category | flops | bytes accessed | tf_op | source)
XLA Modules:
  0.0 776.1 jit_solution(7831380215629716683)
XLA Ops:
  8.5 44.6 %collective-permute-done.6 = bf16[2816,352]{0,1:T(8,128)(2,1)S(1)} collective-permute-done((bf16[2816,352]{0,1:T(8,128)(2,1)}, bf16[2816,352]{0,1:T(8,128)(2,1)S(1)}, u32[]{:S(2)}, u32[]{:S(2)}) %collective-permute-start.6) | collective-permute-done | bytes 1982496 | tf_op jit(solution)/shard_map/ppermute | solution.py:16
  63.9 68.2 %collective-permute-done.7 = bf16[2816,352]{0,1:T(8,128)(2,1)} collective-permute-done((bf16[2816,352]{0,1:T(8,128)(2,1)S(1)}, bf16[2816,352]{0,1:T(8,128)(2,1)}, u32[]{:S(2)}, u32[]{:S(2)}) %collective-permute-start.7) | collective-permute-done | bytes 1982496 | tf_op jit(solution)/shard_map/ppermute | solution.py:16
  132.1 10.1 %collective-permute-start.8 = (bf16[2816,352]{0,1:T(8,128)(2,1)}, bf16[2816,352]{0,1:T(8,128)(2,1)}, u32[]{:S(2)}, u32[]{:S(2)}) collective-permute-start(bf16[2816,352]{0,1:T(8,128)(2,1)} %collective-permute-done.7), channel_id=1, source_target_pairs={{0,4},{4,8},{8,12},{12,16},{16,20},{20,24},{24,28},{28,0},{1,5},{5... | collective-permute-start | bytes 5947400 | tf_op jit(solution)/shard_map/ppermute | solution.py:16
  142.9 13.0 %fusion.108 = (f32[2,16,16]{2,1,0:T(8,128)S(1)}, f32[2,16,16,704]{3,2,1,0:T(8,128)S(1)}) fusion(f32[704]{0:T(1024)S(1)} %get-tuple-element.123, f32[704]{0:T(1024)S(1)} %get-tuple-element.124, f32[704]{0:T(1024)} %get-tuple-element.77, f32[704]{0:T(1024)} %get-tuple-element.78, f32[704]{0:T(1024)} %get-tuple-element.79, f32[704]{0:T(1024)} %get-tuple-element.80, ...), kind=kLoop, calls=%fused_computation.361 | loop fusion | flops 35323392 | bytes 3023616 | tf_op jit(solution)/shard_map/reduce_sum | solution.py:88
  156.3 8.9 %psum.28 = f32[512]{0:T(512)S(1)} all-reduce(f32[512]{0:T(512)S(1)} %reduce_sum.509), channel_id=1, replica_groups=mesh['dp'=8,'chan'=4] {'chan'}, use_global_device_ids=true, to_apply=%region_1.2 | all-reduce | flops 512 | bytes 4096 | tf_op jit(solution)/shard_map/psum | solution.py:88
  165.3 44.7 %collective-permute-done.8 = bf16[2816,352]{0,1:T(8,128)(2,1)} collective-permute-done((bf16[2816,352]{0,1:T(8,128)(2,1)}, bf16[2816,352]{0,1:T(8,128)(2,1)}, u32[]{:S(2)}, u32[]{:S(2)}) %collective-permute-start.8) | collective-permute-done | bytes 1982496 | tf_op jit(solution)/shard_map/ppermute | solution.py:16
  210.0 13.5 %collective-permute-start.9 = (bf16[2816,352]{0,1:T(8,128)(2,1)}, bf16[2816,352]{0,1:T(8,128)(2,1)}, u32[]{:S(2)}, u32[]{:S(2)}) collective-permute-start(bf16[2816,352]{0,1:T(8,128)(2,1)} %collective-permute-done.8), channel_id=1, source_target_pairs={{0,4},{4,8},{8,12},{12,16},{16,20},{20,24},{24,28},{28,0},{1,5},{5... | collective-permute-start | bytes 5947400 | tf_op jit(solution)/shard_map/ppermute | solution.py:16
  223.9 9.2 %psum.29 = f32[512]{0:T(512)S(1)} all-reduce(f32[512]{0:T(512)S(1)} %reduce_sum.511), channel_id=1, replica_groups=mesh['dp'=8,'chan'=4] {'chan'}, use_global_device_ids=true, to_apply=%region_3.4 | all-reduce | flops 512 | bytes 4096 | tf_op jit(solution)/shard_map/psum | solution.py:90
  236.1 16.7 %collective-permute-done.1 = bf16[512,704]{0,1:T(8,128)(2,1)S(1)} collective-permute-done((bf16[512,704]{0,1:T(8,128)(2,1)S(1)}, bf16[512,704]{0,1:T(8,128)(2,1)S(1)}, u32[]{:S(2)}, u32[]{:S(2)}) %collective-permute-start.1) | collective-permute-done | bytes 720928 | tf_op jit(solution)/shard_map/ppermute | solution.py:47
  286.1 8.7 %dynamic_update_slice.29 = bf16[512,2816]{1,0:T(8,128)(2,1)} dynamic-update-slice(bf16[512,2816]{1,0:T(8,128)(2,1)} %dynamic_update_slice.28, bf16[512,704]{1,0:T(8,128)(2,1)S(1)} %copy.23, s32[]{:T(128)} %constant.51.clone.1, s32[]{:T(128)S(6)} %select_n.38) | dynamic-update-slice | bytes 1441796 | tf_op jit(solution)/shard_map/dynamic_update_slice | solution.py:49
  329.7 9.5 %collective-permute-start.12 = (bf16[2816,352]{0,1:T(8,128)(2,1)}, bf16[2816,352]{0,1:T(8,128)(2,1)S(1)}, u32[]{:S(2)}, u32[]{:S(2)}) collective-permute-start(bf16[2816,352]{0,1:T(8,128)(2,1)} %collective-permute-done.11), channel_id=1, source_target_pairs={{0,28},{4,0},{8,4},{12,8},{16,12},{20,16},{24,20},{28,24},{1,29},{... | collective-permute-start | bytes 5947400 | tf_op jit(solution)/shard_map/ppermute | solution.py:18
  349.9 11.9 %collective-permute-done.12 = bf16[2816,352]{0,1:T(8,128)(2,1)S(1)} collective-permute-done((bf16[2816,352]{0,1:T(8,128)(2,1)}, bf16[2816,352]{0,1:T(8,128)(2,1)S(1)}, u32[]{:S(2)}, u32[]{:S(2)}) %collective-permute-start.12) | collective-permute-done | bytes 1982496 | tf_op jit(solution)/shard_map/ppermute | solution.py:18
  380.3 15.3 %multiply_convert_fusion = (bf16[512,2816]{1,0:T(8,128)(2,1)S(1)}, f32[512,2816]{1,0:T(8,128)}) fusion(bf16[512,2816]{1,0:T(8,128)(2,1)} %dynamic_update_slice.27, bf16[2816,2816]{1,0:T(8,128)(2,1)} %all-gather.2.cloned.1.call-done), kind=kOutput, calls=%fused_computation.105 | convolution fusion | flops 8127381504 | bytes 27394048 | tf_op jit(solution)/shard_map/dot_general | solution.py:96
  397.1 11.9 %convolution_convert_fusion.1 = bf16[2816,2816]{1,0:T(8,128)(2,1)} fusion(bf16[512,2816]{1,0:T(8,128)(2,1)S(1)} %copy-done.15, bf16[512,2816]{1,0:T(8,128)(2,1)S(1)} %get-tuple-element.15), kind=kOutput, calls=%fused_computation.97 | convolution fusion | flops 8128102400 | bytes 21626880 | tf_op jit(solution)/shard_map/dot_general | solution.py:101
  409.3 14.4 %fusion.5 = bf16[512,2816]{1,0:T(8,128)(2,1)S(1)} fusion(f32[512,2816]{1,0:T(8,128)} %get-tuple-element.140, bf16[512,2816]{1,0:T(8,128)(2,1)S(1)} %copy-done.15, bf16[2816,2816]{0,1:T(8,128)(2,1)} %constant_dynamic-slice_fusion.6), kind=kOutput, calls=%fused_computation.104 | convolution fusion | flops 8134590464 | bytes 27394048 | tf_op jit(solution)/shard_map/dot_general | solution.py:107
  425.3 11.9 %convolution_convert_fusion = bf16[2816,2816]{1,0:T(8,128)(2,1)} fusion(bf16[512,2816]{1,0:T(8,128)(2,1)S(1)} %copy-done.16, bf16[512,2816]{1,0:T(8,128)(2,1)S(1)} %fusion.5), kind=kOutput, calls=%fused_computation.96 | convolution fusion | flops 8128102400 | bytes 21626880 | tf_op jit(solution)/shard_map/dot_general | solution.py:112
  439.1 13.0 %convolution_convert_fusion.3 = bf16[512,2816]{1,0:T(8,128)(2,1)S(1)} fusion(bf16[512,2816]{1,0:T(8,128)(2,1)S(1)} %copy-done.95, bf16[2816,2816]{0,1:T(8,128)(2,1)} %constant_dynamic-slice_fusion.6), kind=kOutput, calls=%fused_computation.108 | convolution fusion | flops 8121614336 | bytes 21626880 | tf_op jit(solution)/shard_map/dot_general | solution.py:123
  459.7 13.5 %convolution_convert_fusion.2 = bf16[512,2816]{1,0:T(8,128)(2,1)S(1)} fusion(bf16[512,2816]{1,0:T(8,128)(2,1)} %copy-done.96, bf16[2816,2816]{1,0:T(8,128)(2,1)} %all-gather.2.cloned.1.call-done), kind=kOutput, calls=%fused_computation.107 | convolution fusion | flops 8121614336 | bytes 21626880 | tf_op jit(solution)/shard_map/dot_general | solution.py:119
  487.7 28.4 %collective-permute-done.17 = bf16[512,704]{0,1:T(8,128)(2,1)S(1)} collective-permute-done((bf16[512,704]{0,1:T(8,128)(2,1)S(1)}, bf16[512,704]{0,1:T(8,128)(2,1)S(1)}, u32[]{:S(2)}, u32[]{:S(2)}) %collective-permute-start.17) | collective-permute-done | bytes 720928 | tf_op jit(solution)/shard_map/ppermute | solution.py:60
  526.6 9.3 %all-reduce.2 = (f32[512]{0:T(512)S(1)}, f32[512]{0:T(512)S(1)}) all-reduce(f32[512]{0:T(512)S(1)} %get-tuple-element.143, f32[512]{0:T(512)S(1)} %get-tuple-element.142), channel_id=1, replica_groups=mesh['dp'=8,'chan'=4] {'chan'}, use_global_device_ids=true, to_apply=%region_7.8 | all-reduce | flops 1024 | bytes 8192 | tf_op jit(solution)/shard_map/psum | solution.py:131
  556.5 15.3 %collective-permute-start.20 = (f32[52,704]{1,0:T(8,128)S(1)}, f32[52,704]{1,0:T(8,128)S(1)}, u32[]{:S(2)}, u32[]{:S(2)}) collective-permute-start(f32[52,704]{1,0:T(8,128)S(1)} %fusion.121), channel_id=1, source_target_pairs={{0,8},{4,12},{8,0},{12,4},{16,24},{20,28},{24,16},{28,20},{1,9},{5... | collective-permute-start | bytes 439304 | tf_op jit(solution)/shard_map/ppermute | solution.py:72
  571.8 10.5 %collective-permute-done.20 = f32[52,704]{1,0:T(8,128)S(1)} collective-permute-done((f32[52,704]{1,0:T(8,128)S(1)}, f32[52,704]{1,0:T(8,128)S(1)}, u32[]{:S(2)}, u32[]{:S(2)}) %collective-permute-start.20) | collective-permute-done | bytes 146464 | tf_op jit(solution)/shard_map/ppermute | solution.py:72
  587.8 13.3 %fusion.99 = bf16[2,16,16,704]{3,2,1,0:T(8,128)(2,1)} fusion(f32[2,16,16,704]{3,2,1,0:T(8,128)S(1)} %bitcast.104, bf16[2,16,16,704]{3,2,1,0:T(8,128)(2,1)S(1)} %copy-done.9, f32[704]{0:T(1024)S(1)} %copy-done.60, f32[704]{0:T(1024)S(1)} %copy-done.62, f32[704]{0:T(1024)S(1)} %copy-done.23, f32[704]{0:T(1024)S(1)} %copy-done.24, f32[704]{0:T(1024)S(1)} %copy-done.25, ...), kind=kLoop, calls=%fused_computation.203 | loop fusion | flops 36044800 | bytes 3021568 | tf_op jit(solution)/shard_map/convert_element_type | solution.py:159
  609.0 156.6 %reduce-scatter.3.cloned.1.call-done = bf16[352,2816]{1,0:T(8,128)(2,1)} async-done(((bf16[2816,2816]{1,0:T(8,128)(2,1)}), bf16[352,2816]{1,0:T(8,128)(2,1)}) %reduce-scatter.3.cloned.1.call-update) | async-done | bytes 1982480 | tf_op jit(solution)/shard_map/reduce_scatter | solution.py:65
  (376 shorter events, 187.5 us)
Async XLA Ops:
  7.2 373.1 %all-gather.2.cloned.1.call-start = ((), (), s32[]{:S(2)}) async-start(), calls=%async_computation.2 | async-start | bytes 17842176 | tf_op jit(solution)/shard_map/all_gather | solution.py:95
  7.9 597.3 %reduce-scatter.5.cloned.1.call-start = ((), (), s32[]{:S(2)}) async-start(), calls=%async_computation.4 | async-start | bytes 17842176 | tf_op jit(solution)/shard_map/reduce_scatter | solution.py:65
  8.0 45.1 %collective-permute-start.6 = (bf16[2816,352]{0,1:T(8,128)(2,1)}, bf16[2816,352]{0,1:T(8,128)(2,1)S(1)}, u32[]{:S(2)}, u32[]{:S(2)}) collective-permute-start(bf16[2816,352]{0,1:T(8,128)(2,1)} %param.13), channel_id=1, source_target_pairs={{0,4},{4,8},{8,12},{12,16},{16,20},{20,24},{24,28},{28,0},{1,5},{5... | collective-permute-start | bytes 5947400 | tf_op jit(solution)/shard_map/ppermute | solution.py:16
  53.1 79.0 %collective-permute-start.7 = (bf16[2816,352]{0,1:T(8,128)(2,1)S(1)}, bf16[2816,352]{0,1:T(8,128)(2,1)}, u32[]{:S(2)}, u32[]{:S(2)}) collective-permute-start(bf16[2816,352]{0,1:T(8,128)(2,1)S(1)} %collective-permute-done.6), channel_id=1, source_target_pairs={{0,4},{4,8},{8,12},{12,16},{16,20},{20,24},{24,28},{28,0},{1,5},{5... | collective-permute-start | bytes 5947400 | tf_op jit(solution)/shard_map/ppermute | solution.py:16
  54.6 110.7 %collective-permute-start.10 = (bf16[2816,352]{0,1:T(8,128)(2,1)}, bf16[2816,352]{0,1:T(8,128)(2,1)}, u32[]{:S(2)}, u32[]{:S(2)}) collective-permute-start(bf16[2816,352]{0,1:T(8,128)(2,1)} %param.13), channel_id=1, source_target_pairs={{0,28},{4,0},{8,4},{12,8},{16,12},{20,16},{24,20},{28,24},{1,29},{... | collective-permute-start | bytes 5947400 | tf_op jit(solution)/shard_map/ppermute | solution.py:18
  58.6 176.0 %collective-permute-start.3 = (bf16[512,704]{0,1:T(8,128)(2,1)}, bf16[512,704]{0,1:T(8,128)(2,1)}, u32[]{:S(2)}, u32[]{:S(2)}) collective-permute-start(bf16[512,704]{0,1:T(8,128)(2,1)} %copy.22), channel_id=1, source_target_pairs={{0,1},{1,0},{2,3},{3,2},{4,5},{5,4},{6,7},{7,6},{8,9},{9,8},{10,11... | collective-permute-start | bytes 2162696 | tf_op jit(solution)/shard_map/ppermute | solution.py:47
  132.1 77.9 %collective-permute-start.8 = (bf16[2816,352]{0,1:T(8,128)(2,1)}, bf16[2816,352]{0,1:T(8,128)(2,1)}, u32[]{:S(2)}, u32[]{:S(2)}) collective-permute-start(bf16[2816,352]{0,1:T(8,128)(2,1)} %collective-permute-done.7), channel_id=1, source_target_pairs={{0,4},{4,8},{8,12},{12,16},{16,20},{20,24},{24,28},{28,0},{1,5},{5... | collective-permute-start | bytes 5947400 | tf_op jit(solution)/shard_map/ppermute | solution.py:16
  165.3 164.4 %collective-permute-start.11 = (bf16[2816,352]{0,1:T(8,128)(2,1)}, bf16[2816,352]{0,1:T(8,128)(2,1)}, u32[]{:S(2)}, u32[]{:S(2)}) collective-permute-start(bf16[2816,352]{0,1:T(8,128)(2,1)} %collective-permute-done.10), channel_id=1, source_target_pairs={{0,28},{4,0},{8,4},{12,8},{16,12},{20,16},{24,20},{28,24},{1,29},{... | collective-permute-start | bytes 5947400 | tf_op jit(solution)/shard_map/ppermute | solution.py:18
  210.0 129.2 %collective-permute-start.9 = (bf16[2816,352]{0,1:T(8,128)(2,1)}, bf16[2816,352]{0,1:T(8,128)(2,1)}, u32[]{:S(2)}, u32[]{:S(2)}) collective-permute-start(bf16[2816,352]{0,1:T(8,128)(2,1)} %collective-permute-done.8), channel_id=1, source_target_pairs={{0,4},{4,8},{8,12},{12,16},{16,20},{20,24},{24,28},{28,0},{1,5},{5... | collective-permute-start | bytes 5947400 | tf_op jit(solution)/shard_map/ppermute | solution.py:16
  233.7 19.0 %collective-permute-start.1 = (bf16[512,704]{0,1:T(8,128)(2,1)S(1)}, bf16[512,704]{0,1:T(8,128)(2,1)S(1)}, u32[]{:S(2)}, u32[]{:S(2)}) collective-permute-start(bf16[512,704]{0,1:T(8,128)(2,1)S(1)} %copy.16), channel_id=1, source_target_pairs={{0,2},{1,3},{2,0},{3,1},{4,6},{5,7},{6,4},{7,5},{8,10},{9,11},{10,... | collective-permute-start | bytes 2162696 | tf_op jit(solution)/shard_map/ppermute | solution.py:47
  234.3 18.7 %collective-permute-start = (bf16[512,704]{0,1:T(8,128)(2,1)S(1)}, bf16[512,704]{0,1:T(8,128)(2,1)}, u32[]{:S(2)}, u32[]{:S(2)}) collective-permute-start(bf16[512,704]{0,1:T(8,128)(2,1)S(1)} %copy.16), channel_id=1, source_target_pairs={{0,1},{1,0},{2,3},{3,2},{4,5},{5,4},{6,7},{7,6},{8,9},{9,8},{10,11... | collective-permute-start | bytes 2162696 | tf_op jit(solution)/shard_map/ppermute | solution.py:47
  234.6 68.2 %collective-permute-start.4 = (bf16[512,704]{0,1:T(8,128)(2,1)}, bf16[512,704]{0,1:T(8,128)(2,1)}, u32[]{:S(2)}, u32[]{:S(2)}) collective-permute-start(bf16[512,704]{0,1:T(8,128)(2,1)} %copy.22), channel_id=1, source_target_pairs={{0,2},{1,3},{2,0},{3,1},{4,6},{5,7},{6,4},{7,5},{8,10},{9,11},{10,... | collective-permute-start | bytes 2162696 | tf_op jit(solution)/shard_map/ppermute | solution.py:47
  252.7 59.3 %collective-permute-start.2 = (bf16[512,704]{0,1:T(8,128)(2,1)S(1)}, bf16[512,704]{0,1:T(8,128)(2,1)}, u32[]{:S(2)}, u32[]{:S(2)}) collective-permute-start(bf16[512,704]{0,1:T(8,128)(2,1)S(1)} %copy.16), channel_id=1, source_target_pairs={{0,3},{1,2},{2,1},{3,0},{4,7},{5,6},{6,5},{7,4},{8,11},{9,10},{10,... | collective-permute-start | bytes 2162696 | tf_op jit(solution)/shard_map/ppermute | solution.py:47
  253.0 68.4 %collective-permute-start.5 = (bf16[512,704]{0,1:T(8,128)(2,1)}, bf16[512,704]{0,1:T(8,128)(2,1)S(1)}, u32[]{:S(2)}, u32[]{:S(2)}) collective-permute-start(bf16[512,704]{0,1:T(8,128)(2,1)} %copy.22), channel_id=1, source_target_pairs={{0,3},{1,2},{2,1},{3,0},{4,7},{5,6},{6,5},{7,4},{8,11},{9,10},{10,... | collective-permute-start | bytes 2162696 | tf_op jit(solution)/shard_map/ppermute | solution.py:47
  329.7 32.2 %collective-permute-start.12 = (bf16[2816,352]{0,1:T(8,128)(2,1)}, bf16[2816,352]{0,1:T(8,128)(2,1)S(1)}, u32[]{:S(2)}, u32[]{:S(2)}) collective-permute-start(bf16[2816,352]{0,1:T(8,128)(2,1)} %collective-permute-done.11), channel_id=1, source_target_pairs={{0,28},{4,0},{8,4},{12,8},{16,12},{20,16},{24,20},{28,24},{1,29},{... | collective-permute-start | bytes 5947400 | tf_op jit(solution)/shard_map/ppermute | solution.py:18
  409.1 356.6 %reduce-scatter.3.cloned.1.call-start = ((), (), s32[]{:S(2)}) async-start(), calls=%async_computation.3 | async-start | bytes 17842176 | tf_op jit(solution)/shard_map/reduce_scatter | solution.py:65
  456.2 24.0 %collective-permute-start.14 = (bf16[512,704]{0,1:T(8,128)(2,1)}, bf16[512,704]{0,1:T(8,128)(2,1)}, u32[]{:S(2)}, u32[]{:S(2)}) collective-permute-start(bf16[512,704]{0,1:T(8,128)(2,1)} %copy.30), channel_id=1, source_target_pairs={{0,2},{1,3},{2,0},{3,1},{4,6},{5,7},{6,4},{7,5},{8,10},{9,11},{10,... | collective-permute-start | bytes 2162696 | tf_op jit(solution)/shard_map/ppermute | solution.py:60
  457.2 26.0 %collective-permute-start.15 = (bf16[512,704]{0,1:T(8,128)(2,1)}, bf16[512,704]{0,1:T(8,128)(2,1)}, u32[]{:S(2)}, u32[]{:S(2)}) collective-permute-start(bf16[512,704]{0,1:T(8,128)(2,1)} %copy.32), channel_id=1, source_target_pairs={{0,3},{1,2},{2,1},{3,0},{4,7},{5,6},{6,5},{7,4},{8,11},{9,10},{10,... | collective-permute-start | bytes 2162696 | tf_op jit(solution)/shard_map/ppermute | solution.py:60
  459.0 26.4 %collective-permute-start.13 = (bf16[512,704]{0,1:T(8,128)(2,1)S(1)}, bf16[512,704]{0,1:T(8,128)(2,1)}, u32[]{:S(2)}, u32[]{:S(2)}) collective-permute-start(bf16[512,704]{0,1:T(8,128)(2,1)S(1)} %copy.28), channel_id=1, source_target_pairs={{0,1},{1,0},{2,3},{3,2},{4,5},{5,4},{6,7},{7,6},{8,9},{9,8},{10,11... | collective-permute-start | bytes 2162696 | tf_op jit(solution)/shard_map/ppermute | solution.py:60
  476.2 40.0 %collective-permute-start.17 = (bf16[512,704]{0,1:T(8,128)(2,1)S(1)}, bf16[512,704]{0,1:T(8,128)(2,1)S(1)}, u32[]{:S(2)}, u32[]{:S(2)}) collective-permute-start(bf16[512,704]{0,1:T(8,128)(2,1)S(1)} %copy.36), channel_id=1, source_target_pairs={{0,2},{1,3},{2,0},{3,1},{4,6},{5,7},{6,4},{7,5},{8,10},{9,11},{10,... | collective-permute-start | bytes 2162696 | tf_op jit(solution)/shard_map/ppermute | solution.py:60
  478.4 38.9 %collective-permute-start.18 = (bf16[512,704]{0,1:T(8,128)(2,1)}, bf16[512,704]{0,1:T(8,128)(2,1)S(1)}, u32[]{:S(2)}, u32[]{:S(2)}) collective-permute-start(bf16[512,704]{0,1:T(8,128)(2,1)} %copy.38), channel_id=1, source_target_pairs={{0,3},{1,2},{2,1},{3,0},{4,7},{5,6},{6,5},{7,4},{8,11},{9,10},{10,... | collective-permute-start | bytes 2162696 | tf_op jit(solution)/shard_map/ppermute | solution.py:60
  480.2 38.3 %collective-permute-start.16 = (bf16[512,704]{0,1:T(8,128)(2,1)}, bf16[512,704]{0,1:T(8,128)(2,1)}, u32[]{:S(2)}, u32[]{:S(2)}) collective-permute-start(bf16[512,704]{0,1:T(8,128)(2,1)} %copy.34), channel_id=1, source_target_pairs={{0,1},{1,0},{2,3},{3,2},{4,5},{5,4},{6,7},{7,6},{8,9},{9,8},{10,11... | collective-permute-start | bytes 2162696 | tf_op jit(solution)/shard_map/ppermute | solution.py:60
  556.5 25.8 %collective-permute-start.20 = (f32[52,704]{1,0:T(8,128)S(1)}, f32[52,704]{1,0:T(8,128)S(1)}, u32[]{:S(2)}, u32[]{:S(2)}) collective-permute-start(f32[52,704]{1,0:T(8,128)S(1)} %fusion.121), channel_id=1, source_target_pairs={{0,8},{4,12},{8,0},{12,4},{16,24},{20,28},{24,16},{28,20},{1,9},{5... | collective-permute-start | bytes 439304 | tf_op jit(solution)/shard_map/ppermute | solution.py:72
  582.4 20.7 %collective-permute-start.21 = (f32[52,704]{1,0:T(8,128)S(1)}, f32[52,704]{1,0:T(8,128)S(1)}, u32[]{:S(2)}, u32[]{:S(2)}) collective-permute-start(f32[52,704]{1,0:T(8,128)S(1)} %add.511), channel_id=1, source_target_pairs={{0,16},{4,20},{8,24},{12,28},{16,0},{20,4},{24,8},{28,12},{1,17},{... | collective-permute-start | bytes 439304 | tf_op jit(solution)/shard_map/ppermute | solution.py:72
  (98 other events, 2448.0 us)
Sparse Core Ops, SparseCore 0:
  9.7 242.2 all-gather.1
  409.2 196.0 reduce-scatter.4
  607.6 157.9 reduce-scatter.2
